TPU v7x, 512 devices: a whole 4x4x16 slice. The times are simulated.
512 devices in a mesh: seq: 8 (over y, core), expert: 64 (over z, x).
Axes of the slice: x: 4, y: 4, z: 16, core: 2. Of those that a mesh axis runs over, the one named last changes fastest.
Arguments:
- tokens: bfloat16 [65536, 2048], P(('seq', 'expert')), may hold values from -4 to 4
- routes: int32 [65536, 8], P(('seq', 'expert')), may hold values from 0 to 127, all different within a row; in each aligned block of 128 rows (0 to 127, 128 to 255, ...) at most 16 rows name the same one
- gate_shares: int32 [65536, 8], P(('seq', 'expert')), may hold values from 1 to 65536
- gate_up: bfloat16 [128, 2048, 768], P('expert', 'seq'), may hold values from -0.125 to 0.125
Outputs:
- gram: float32 [128, 384, 384], P('expert', 'seq')
- maxima: float32 [128, 2048], P('expert', 'seq')
Inputs may be any that keep to these rules, and one draw needn't show every extreme that they name: `routes`: among the 128 rows of one device no expert is named more than 16 times.
All inputs are finite; a program needn't handle non-finite values.
Results may differ from a plain program's by a relative error of at most 0.0049.
Values may be sent and summed in bfloat16 or wider, within the bound.
A program may use at most 64 MiB of HBM per device.

v0:
```python
import jax
import jax.numpy as jnp
from jax import lax
from jax.sharding import PartitionSpec as P

D = 2048
FWIN = 384


def hidden_of(projected):
    return (jax.nn.silu(projected[..., :FWIN]) * projected[..., FWIN:]).astype(jnp.bfloat16)


def split_weighted(hidden, row_shares):
    weighted = hidden.astype(jnp.float32) * row_shares[..., None]
    weighted_high = weighted.astype(jnp.bfloat16)
    weighted_low = (weighted - weighted_high.astype(jnp.float32)).astype(jnp.bfloat16)
    return (weighted_high, weighted_low)


def body(tokens, routes, gate_shares, gate_up):
    tok_rows = tokens.shape[0]
    top_count = routes.shape[1]
    expert_count = lax.axis_size("expert")
    seq_count = lax.axis_size("seq")
    local_count = gate_up.shape[0]
    all_experts = local_count * expert_count
    capacity = 2 * tok_rows * top_count // all_experts
    norm_factor = all_experts / (tok_rows * seq_count * expert_count * top_count)
    chosen = routes.reshape(-1)
    shares = gate_shares.reshape(-1).astype(jnp.float32) / 65536.0
    one_hot = (chosen[:, None] == jnp.arange(all_experts, dtype=jnp.int32)[None, :]).astype(
        jnp.int32
    )
    ranked = jnp.sum((jnp.cumsum(one_hot, axis=0) - one_hot) * one_hot, axis=1)
    slot_index = chosen * capacity + ranked
    token_index = jnp.arange(tok_rows * top_count, dtype=jnp.int32) // top_count
    outgoing_rows = (
        jnp.zeros((all_experts * capacity, D), jnp.bfloat16).at[slot_index].set(tokens[token_index])
    )
    out_shares = jnp.zeros((all_experts * capacity,), jnp.float32).at[slot_index].set(shares)
    outgoing_rows = outgoing_rows.reshape(expert_count, local_count, capacity, D)
    out_shares = out_shares.reshape(expert_count, local_count, capacity)
    arrived, arrived_shares = (
        lax.all_to_all(outgoing_rows, "expert", split_axis=0, concat_axis=0, tiled=True),
        lax.all_to_all(
            out_shares.astype(jnp.bfloat16), "expert", split_axis=0, concat_axis=0, tiled=True
        ).astype(out_shares.dtype),
    )
    is_live = arrived_shares > 0.0
    channel_max = jnp.max(jnp.where(is_live[..., None], jnp.abs(arrived), 0), axis=(0, 2)).astype(
        jnp.float32
    )
    projected = jnp.einsum(
        "slcd,ldf->lscf",
        arrived,
        lax.all_gather(gate_up, "seq", axis=1, tiled=True),
        preferred_element_type=jnp.float32,
    )
    hidden = hidden_of(projected).reshape(local_count, expert_count * capacity, FWIN)
    row_shares = jnp.transpose(arrived_shares, (1, 0, 2)).reshape(
        local_count, expert_count * capacity
    )
    weighted_high, weighted_low = split_weighted(hidden, row_shares)
    gram_part = jnp.einsum(
        "lrf,lrg->lfg", hidden, weighted_high, preferred_element_type=jnp.float32
    )
    gram_part = gram_part + jnp.einsum(
        "lrf,lrg->lfg", hidden, weighted_low, preferred_element_type=jnp.float32
    )
    gram_part = gram_part * norm_factor
    gram = lax.psum_scatter(gram_part, "seq", scatter_dimension=1, tiled=True)
    full_max = lax.pmax(channel_max, "seq")
    slice_width = D // seq_count
    maxima = lax.dynamic_slice_in_dim(full_max, lax.axis_index("seq") * slice_width, slice_width, 1)
    return (gram, maxima)


def solution(mesh):
    return jax.shard_map(
        body,
        mesh=mesh,
        in_specs=(
            P(("seq", "expert"), None),
            P(("seq", "expert"), None),
            P(("seq", "expert"), None),
            P("expert", "seq", None),
        ),
        out_specs=(P("expert", "seq", None), P("expert", "seq")),
        check_vma=False,
    )
```

profile of v0, /device:TPU:2, one launch (start us, length us, event | category | flops | bytes accessed | tf_op | source)
XLA Modules:
  0.0 496.8 jit_solution(5624225172314754121)
XLA Ops:
  7.2 0.8 copy.20
  8.2 0.7 broadcast_multiply_fusion
  8.9 0.1 copy.22
  9.0 0.2 fusion.21
  9.3 0.1 copy.23
  9.4 0.1 copy.19
  9.6 0.1 copy.25
  9.8 0.4 fusion.20
  10.2 4.3 scatter_custom_fusion.1
  14.6 0.7 convert_element_type.46
  15.3 18.6 %all-to-all-start.1 = ((bf16[64,2,16]{2,1,0:T(2,128)(2,1)}), bf16[64,2,16]{2,1,0:T(2,128)(2,1)S(1)}, u32[]{:S(2)}, u32[]{:S(2)}) async-start(bf16[64,2,16]{2,1,0:T(2,128)(2,1)} %convert_element_type.46), calls=%async_computation.1 | async-start | bytes 65536 | tf_op jit(solution)/shard_map/all_to_all | solution.py:46
  34.0 24.9 %scatter_custom_fusion = bf16[2048,2048]{1,0:T(8,128)(2,1)} fusion(s32[1024]{0:T(1024)S(1)} %bitcast.30, bf16[128,2048]{1,0:T(8,128)(2,1)S(1)} %copy-done, s32[1024]{0:T(1024)S(1)} %broadcast_clamp_fusion, bf16[]{:T(256)} %constant.19.clone.1), kind=kCustom, calls=%fused_computation.7 | custom fusion | bytes 8388610 | tf_op jit(solution)/shard_map/scatter | solution.py:39
  58.9 15.3 %all-to-all-start = ((bf16[64,2,16,2048]{3,2,1,0:T(8,128)(2,1)}), bf16[64,2,16,2048]{3,2,1,0:T(8,128)(2,1)}, u32[]{:S(2)}, u32[]{:S(2)}) async-start(bf16[64,2,16,2048]{3,2,1,0:T(8,128)(2,1)} %bitcast.24), calls=%async_computation | async-start | bytes 16777216 | tf_op jit(solution)/shard_map/all_to_all | solution.py:45
  74.2 0.7 all-gather.2.cloned.1.call-update
  75.1 51.5 %all-gather.2.cloned.1.call-done = bf16[2,2048,768]{2,1,0:T(8,128)(2,1)} async-done(((bf16[2,256,768]{2,1,0:T(8,128)(2,1)}), bf16[2,2048,768]{2,1,0:T(8,128)(2,1)}) %all-gather.2.cloned.1.call-update) | async-done | bytes 6291472 | tf_op jit(solution)/shard_map/all_gather | solution.py:57
  126.6 316.8 %all-to-all-done = bf16[64,2,16,2048]{3,2,1,0:T(8,128)(2,1)} async-done(((bf16[64,2,16,2048]{3,2,1,0:T(8,128)(2,1)}), bf16[64,2,16,2048]{3,2,1,0:T(8,128)(2,1)}, u32[]{:S(2)}, u32[]{:S(2)}) %all-to-all-start) | async-done | bytes 8388640 | tf_op jit(solution)/shard_map/all_to_all | solution.py:45
  443.3 10.0 %fusion = f32[2,64,16,768]{3,2,1,0:T(8,128)S(1)} fusion(bf16[64,2,16,2048]{3,2,1,0:T(8,128)(2,1)} %all-to-all-done, bf16[2,2048,768]{2,1,0:T(8,128)(2,1)} %all-gather.2.cloned.1.call-done), kind=kOutput, calls=%fused_computation.3 | convolution fusion | flops 6442450944 | bytes 20971520 | tf_op jit(solution)/shard_map/slcd,ldf->lscf/dot_general | solution.py:54
  453.4 0.9 fusion.6
  454.3 1.2 fusion.10
  455.5 2.3 fusion.16
  458.0 5.2 %select_reduce_fusion = bf16[2,2048]{1,0:T(2,128)(2,1)S(1)} fusion(bf16[64,2,16,2048]{3,2,1,0:T(8,128)(2,1)} %all-to-all-done, pred[64,2,16]{2,1,0:T(4,128)(4,1)S(1)} %convert_compare_fusion), kind=kLoop, calls=%fused_computation.5 | loop fusion | flops 12578816 | bytes 8398848 | tf_op jit(solution)/shard_map/reduce_max | solution.py:51
  463.1 23.7 %pmax.7 = f32[2,2048]{1,0:T(2,128)S(1)} all-reduce(bf16[2,2048]{1,0:T(2,128)(2,1)S(1)} %select_reduce_fusion), channel_id=1, replica_groups=mesh['seq'=8,'expert'=64] {'seq'}, use_global_device_ids=true, to_apply=%region_7.8 | all-reduce | flops 4096 | bytes 24576 | tf_op jit(solution)/shard_map/pmax | solution.py:73
  486.8 0.6 constant_dynamic-slice_fusion
  487.4 2.5 reduce-scatter.2.cloned.1.call-done
  (25 shorter events, 0.8 us)
Async XLA Ops:
  7.2 26.8 %copy-start = (bf16[128,2048]{1,0:T(8,128)(2,1)S(1)}, bf16[128,2048]{1,0:T(8,128)(2,1)}, u32[]{:S(2)}) copy-start(bf16[128,2048]{1,0:T(8,128)(2,1)} %param.4) | copy-start | bytes 1572868
  7.2 2.4 copy-start.1
  15.3 43.6 %all-to-all-start.1 = ((bf16[64,2,16]{2,1,0:T(2,128)(2,1)}), bf16[64,2,16]{2,1,0:T(2,128)(2,1)S(1)}, u32[]{:S(2)}, u32[]{:S(2)}) async-start(bf16[64,2,16]{2,1,0:T(2,128)(2,1)} %convert_element_type.46), calls=%async_computation.1 | async-start | bytes 65536 | tf_op jit(solution)/shard_map/all_to_all | solution.py:46
  58.9 384.4 %all-to-all-start = ((bf16[64,2,16,2048]{3,2,1,0:T(8,128)(2,1)}), bf16[64,2,16,2048]{3,2,1,0:T(8,128)(2,1)}, u32[]{:S(2)}, u32[]{:S(2)}) async-start(bf16[64,2,16,2048]{3,2,1,0:T(8,128)(2,1)} %bitcast.24), calls=%async_computation | async-start | bytes 16777216 | tf_op jit(solution)/shard_map/all_to_all | solution.py:45
  74.2 52.4 %all-gather.2.cloned.1.call-start = ((), (), s32[]{:S(2)}) async-start(), calls=%async_computation.3 | async-start | bytes 7077888 | tf_op jit(solution)/shard_map/all_gather | solution.py:57
  74.9 415.0 %reduce-scatter.2.cloned.1.call-start = ((), (), s32[]{:S(2)}) async-start(), calls=%async_computation.4 | async-start | bytes 1327104 | tf_op jit(solution)/shard_map/reduce_scatter | solution.py:72
Sparse Core Ops, SparseCore 0:
  77.1 49.4 all-gather.1
  458.0 31.8 reduce-scatter.1
where the time goes:
time: 497 us
  waiting for transfers between devices  371 us (75%)
  starting transfers between devices  34 us (7%)
  local copies, waits for them, and re-layouts  32.3 us (6%)
  blocking collectives  23.7 us (5%)
  between operations  14.2 us (3%)
  matrix products  13.6 us (3%)
  other arithmetic  7.54 us (2%)
    all_to_all x1, waiting for transfers between devices, body(): lax.all_to_all(outgoing_rows, 'expert', split_axis=0, concat_axis=0, tile...  317 us
    all_gather x1, waiting for transfers between devices, body(): lax.all_gather(gate_up, 'seq', axis=1, tiled=True)  51.5 us
    scatter x1, local copies, waits for them, and re-layouts, body(): jnp.zeros((all_experts * capacity, D), jnp.bfloat16).at[slot_index]  24.9 us
    pmax x1, blocking collectives, body(): full_max = lax.pmax(channel_max, 'seq')  23.7 us
    all_to_all x1, starting transfers between devices, body(): lax.all_to_all(out_shares.astype(jnp.bfloat16), 'expert', split_axis=0, c...  18.6 us
    all_to_all x1, starting transfers between devices, body(): lax.all_to_all(outgoing_rows, 'expert', split_axis=0, concat_axis=0, tile...  15.3 us
    dot_general x1, matrix products, body(): jnp.einsum('slcd,ldf->lscf', arrived, lax.all_gather(gate_up, 'seq', axis...  10 us
  transfers between devices with their start and end apart: 4, of which 3 were waited for; matrix products, arithmetic and copies ran while one was open for 6% of the time, Pallas kernels for 0%

commit v1 on v0

--- a/solution.py
+++ b/solution.py
@@ -5,6 +5,33 @@
 
 D = 2048
 FWIN = 384
+
+
+def _take_shards(payload):
+    current_block, then, side_arr = (
+        jax.lax.axis_size("seq"),
+        jax.lax.axis_index("seq"),
+        payload.shape[1],
+    )
+    all_rows = [(at, (at + 1) % current_block) for at in range(current_block)]
+    t_next = jnp.zeros(
+        (*payload.shape[:1], current_block * side_arr, *payload.shape[2:]), payload.dtype
+    )
+    trail = [(at, (at - 1) % current_block) for at in range(current_block)]
+    t_next = lax.dynamic_update_slice_in_dim(t_next, payload, then * side_arr, axis=1)
+    local_out = mat_out = payload
+    block_last = current_block // 2
+    for dev_j in range(1, block_last + 1):
+        local_out = jax.lax.ppermute(local_out, axis_name="seq", perm=all_rows)
+        t_next = lax.dynamic_update_slice_in_dim(
+            t_next, local_out, (then - dev_j) % current_block * side_arr, axis=1
+        )
+        if dev_j < current_block - block_last:
+            mat_out = jax.lax.ppermute(mat_out, perm=trail, axis_name="seq")
+            t_next = lax.dynamic_update_slice_in_dim(
+                t_next, mat_out, (then + dev_j) % current_block * side_arr, axis=1
+            )
+    return t_next
 
 
 def hidden_of(projected):
@@ -52,10 +79,7 @@
         jnp.float32
     )
     projected = jnp.einsum(
-        "slcd,ldf->lscf",
-        arrived,
-        lax.all_gather(gate_up, "seq", axis=1, tiled=True),
-        preferred_element_type=jnp.float32,
+        "slcd,ldf->lscf", arrived, _take_shards(gate_up), preferred_element_type=jnp.float32
     )
     hidden = hidden_of(projected).reshape(local_count, expert_count * capacity, FWIN)
     row_shares = jnp.transpose(arrived_shares, (1, 0, 2)).reshape(

time: 497 us -> 498 us (level)
  waiting for transfers between devices: 371 us -> 348 us
  local copies, waits for them, and re-layouts: 32.3 us -> 46.3 us
  starting transfers between devices: 34 us -> 43.4 us
    all_gather x1 -> x0, waiting for transfers between devices: 51.5 us -> none  [body(): lax.all_gather(gate_up, 'seq', axis=1, tiled=True)]
    ppermute x0 -> x7, waiting for transfers between devices: none -> 28.6 us  [the longest x4 28.6 us: _take_shards(): local_out = jax.lax.ppermute(local_out, axis_name='seq', perm=all_rows)]
    dynamic_update_slice x0 -> x8, local copies, waits for them, and re-layouts: none -> 11 us  [the longest x4 6.09 us: _take_shards(): lax.dynamic_update_slice_in_dim(t_next, local_out, (then - dev_j) % curre...]
    ppermute x0 -> x7, starting transfers between devices: none -> 9.3 us  [the longest x3 9.28 us: _take_shards(): mat_out = jax.lax.ppermute(mat_out, perm=trail, axis_name='seq')]
  transfers between devices with their start and end apart: 4 -> 10, of which waited for: 3 -> 6; matrix products, arithmetic and copies ran while one was open for 6% -> 9% of each run, Pallas kernels for 0% -> 0%
where the time goes in v1:
time: 498 us
  waiting for transfers between devices  348 us (70%)
  local copies, waits for them, and re-layouts  46.3 us (9%)
  starting transfers between devices  43.4 us (9%)
  blocking collectives  23.7 us (5%)
  between operations  14.2 us (3%)
  matrix products  13.6 us (3%)
  other arithmetic  8.27 us (2%)
    all_to_all x1, waiting for transfers between devices, body(): lax.all_to_all(outgoing_rows, 'expert', split_axis=0, concat_axis=0, tile...  317 us
    ppermute x4, waiting for transfers between devices, _take_shards(): local_out = jax.lax.ppermute(local_out, axis_name='seq', perm=all_rows)  28.6 us
    scatter x1, local copies, waits for them, and re-layouts, body(): jnp.zeros((all_experts * capacity, D), jnp.bfloat16).at[slot_index]  24.9 us
    pmax x1, blocking collectives, body(): full_max = lax.pmax(channel_max, 'seq')  23.7 us
    all_to_all x1, starting transfers between devices, body(): lax.all_to_all(out_shares.astype(jnp.bfloat16), 'expert', split_axis=0, c...  18.6 us
    all_to_all x1, starting transfers between devices, body(): lax.all_to_all(outgoing_rows, 'expert', split_axis=0, concat_axis=0, tile...  15.4 us
    dot_general x1, matrix products, body(): jnp.einsum('slcd,ldf->lscf', arrived, _take_shards(gate_up), preferred_el...  10 us
  transfers between devices with their start and end apart: 10, of which 6 were waited for; matrix products, arithmetic and copies ran while one was open for 9% of the time, Pallas kernels for 0%

profile of v1, /device:TPU:2, one launch (start us, length us, event | category | flops | bytes accessed | tf_op | source)
XLA Modules:
  0.0 497.6 jit_solution(5991794042135191551)
XLA Ops:
  10.9 4.3 scatter_custom_fusion.1
  15.9 18.6 %all-to-all-start.1 = ((bf16[64,2,16]{2,1,0:T(2,128)(2,1)}), bf16[64,2,16]{2,1,0:T(2,128)(2,1)S(1)}, u32[]{:S(2)}, u32[]{:S(2)}) async-start(bf16[64,2,16]{2,1,0:T(2,128)(2,1)} %convert_element_type.46), calls=%async_computation.1 | async-start | bytes 65536 | tf_op jit(solution)/shard_map/all_to_all | solution.py:73
  34.6 24.9 %scatter_custom_fusion = bf16[2048,2048]{1,0:T(8,128)(2,1)} fusion(s32[1024]{0:T(1024)S(1)} %bitcast.30, bf16[128,2048]{1,0:T(8,128)(2,1)S(1)} %copy-done, s32[1024]{0:T(1024)S(1)} %broadcast_clamp_fusion, bf16[]{:T(256)} %constant.80.clone.1), kind=kCustom, calls=%fused_computation.7 | custom fusion | bytes 8388610 | tf_op jit(solution)/shard_map/scatter | solution.py:66
  59.5 15.4 %all-to-all-start = ((bf16[64,2,16,2048]{3,2,1,0:T(8,128)(2,1)}), bf16[64,2,16,2048]{3,2,1,0:T(8,128)(2,1)}, u32[]{:S(2)}, u32[]{:S(2)}) async-start(bf16[64,2,16,2048]{3,2,1,0:T(8,128)(2,1)} %bitcast.24), calls=%async_computation | async-start | bytes 16777216 | tf_op jit(solution)/shard_map/all_to_all | solution.py:72
  75.0 2.9 collective-permute-start.1
  78.0 9.7 %collective-permute-done = bf16[2,256,768]{2,1,0:T(8,128)(2,1)S(1)} collective-permute-done((bf16[2,256,768]{2,1,0:T(8,128)(2,1)S(1)}, bf16[2,256,768]{2,1,0:T(8,128)(2,1)S(1)}, u32[]{:S(2)}, u32[]{:S(2)}) %collective-permute-start) | collective-permute-done | bytes 786464 | tf_op jit(solution)/shard_map/ppermute | solution.py:25
  87.7 3.4 collective-permute-start.3
  91.0 9.4 %collective-permute-done.2 = bf16[2,256,768]{2,1,0:T(8,128)(2,1)} collective-permute-done((bf16[2,256,768]{2,1,0:T(8,128)(2,1)S(1)}, bf16[2,256,768]{2,1,0:T(8,128)(2,1)}, u32[]{:S(2)}, u32[]{:S(2)}) %collective-permute-start.2) | collective-permute-done | bytes 786464 | tf_op jit(solution)/shard_map/ppermute | solution.py:25
  100.4 3.1 broadcast_in_dim.27
  104.4 3.0 collective-permute-start.5
  107.5 5.8 %collective-permute-done.4 = bf16[2,256,768]{2,1,0:T(8,128)(2,1)} collective-permute-done((bf16[2,256,768]{2,1,0:T(8,128)(2,1)}, bf16[2,256,768]{2,1,0:T(8,128)(2,1)}, u32[]{:S(2)}, u32[]{:S(2)}) %collective-permute-start.4) | collective-permute-done | bytes 786464 | tf_op jit(solution)/shard_map/ppermute | solution.py:25
  115.2 2.1 constant_dynamic-update-slice_fusion.4
  117.3 2.0 constant_dynamic-update-slice_fusion.3
  119.4 2.1 constant_dynamic-update-slice_fusion.2
  121.4 1.0 constant_dynamic-update-slice_fusion.1
  122.4 3.8 collective-permute-done.6
  126.2 1.0 constant_dynamic-update-slice_fusion
  127.2 317.0 %all-to-all-done = bf16[64,2,16,2048]{3,2,1,0:T(8,128)(2,1)} async-done(((bf16[64,2,16,2048]{3,2,1,0:T(8,128)(2,1)}), bf16[64,2,16,2048]{3,2,1,0:T(8,128)(2,1)}, u32[]{:S(2)}, u32[]{:S(2)}) %all-to-all-start) | async-done | bytes 8388640 | tf_op jit(solution)/shard_map/all_to_all | solution.py:72
  444.1 10.0 %fusion = f32[2,64,16,768]{3,2,1,0:T(8,128)S(1)} fusion(bf16[64,2,16,2048]{3,2,1,0:T(8,128)(2,1)} %all-to-all-done, bf16[2,2048,768]{2,1,0:T(8,128)(2,1)} %constant_dynamic-update-slice_fusion), kind=kOutput, calls=%fused_computation.3 | convolution fusion | flops 6442450944 | bytes 20971520 | tf_op jit(solution)/shard_map/slcd,ldf->lscf/dot_general | solution.py:81
  455.1 1.2 fusion.10
  456.3 2.3 fusion.16
  458.7 5.2 %select_reduce_fusion = bf16[2,2048]{1,0:T(2,128)(2,1)S(1)} fusion(bf16[64,2,16,2048]{3,2,1,0:T(8,128)(2,1)} %all-to-all-done, pred[64,2,16]{2,1,0:T(4,128)(4,1)S(1)} %convert_compare_fusion), kind=kLoop, calls=%fused_computation.5 | loop fusion | flops 12578816 | bytes 8398848 | tf_op jit(solution)/shard_map/reduce_max | solution.py:78
  463.9 23.7 %pmax.7 = f32[2,2048]{1,0:T(2,128)S(1)} all-reduce(bf16[2,2048]{1,0:T(2,128)(2,1)S(1)} %select_reduce_fusion), channel_id=1, replica_groups=mesh['seq'=8,'expert'=64] {'seq'}, use_global_device_ids=true, to_apply=%region_7.8 | all-reduce | flops 4096 | bytes 24576 | tf_op jit(solution)/shard_map/pmax | solution.py:97
  488.2 2.5 reduce-scatter.2.cloned.1.call-done
  (44 shorter events, 9.0 us)
Async XLA Ops:
  7.2 27.4 %copy-start = (bf16[128,2048]{1,0:T(8,128)(2,1)S(1)}, bf16[128,2048]{1,0:T(8,128)(2,1)}, u32[]{:S(2)}) copy-start(bf16[128,2048]{1,0:T(8,128)(2,1)} %param.4) | copy-start | bytes 1572868
  15.9 43.6 %all-to-all-start.1 = ((bf16[64,2,16]{2,1,0:T(2,128)(2,1)}), bf16[64,2,16]{2,1,0:T(2,128)(2,1)S(1)}, u32[]{:S(2)}, u32[]{:S(2)}) async-start(bf16[64,2,16]{2,1,0:T(2,128)(2,1)} %convert_element_type.46), calls=%async_computation.1 | async-start | bytes 65536 | tf_op jit(solution)/shard_map/all_to_all | solution.py:73
  59.5 15.5 %copy-start.1 = (bf16[2,256,768]{2,1,0:T(8,128)(2,1)S(1)}, bf16[2,256,768]{2,1,0:T(8,128)(2,1)}, u32[]{:S(2)}) copy-start(bf16[2,256,768]{2,1,0:T(8,128)(2,1)} %param.7) | copy-start | bytes 2359300
  59.5 384.6 %all-to-all-start = ((bf16[64,2,16,2048]{3,2,1,0:T(8,128)(2,1)}), bf16[64,2,16,2048]{3,2,1,0:T(8,128)(2,1)}, u32[]{:S(2)}, u32[]{:S(2)}) async-start(bf16[64,2,16,2048]{3,2,1,0:T(8,128)(2,1)} %bitcast.24), calls=%async_computation | async-start | bytes 16777216 | tf_op jit(solution)/shard_map/all_to_all | solution.py:72
  75.0 415.8 %reduce-scatter.2.cloned.1.call-start = ((), (), s32[]{:S(2)}) async-start(), calls=%async_computation.3 | async-start | bytes 1327104 | tf_op jit(solution)/shard_map/reduce_scatter | solution.py:96
  75.0 12.6 %collective-permute-start = (bf16[2,256,768]{2,1,0:T(8,128)(2,1)S(1)}, bf16[2,256,768]{2,1,0:T(8,128)(2,1)S(1)}, u32[]{:S(2)}, u32[]{:S(2)}) collective-permute-start(bf16[2,256,768]{2,1,0:T(8,128)(2,1)S(1)} %copy-done.1), channel_id=1, source_target_pairs={{0,64},{64,128},{128,192},{192,256},{256,320},{320,384},{384,448},... | collective-permute-start | bytes 2359304 | tf_op jit(solution)/shard_map/ppermute | solution.py:25
  75.0 12.6 %collective-permute-start.1 = (bf16[2,256,768]{2,1,0:T(8,128)(2,1)S(1)}, bf16[2,256,768]{2,1,0:T(8,128)(2,1)S(1)}, u32[]{:S(2)}, u32[]{:S(2)}) collective-permute-start(bf16[2,256,768]{2,1,0:T(8,128)(2,1)S(1)} %copy-done.1), channel_id=1, source_target_pairs={{0,448},{64,0},{128,64},{192,128},{256,192},{320,256},{384,320},{4... | collective-permute-start | bytes 2359304 | tf_op jit(solution)/shard_map/ppermute | solution.py:30
  87.7 12.7 %collective-permute-start.2 = (bf16[2,256,768]{2,1,0:T(8,128)(2,1)S(1)}, bf16[2,256,768]{2,1,0:T(8,128)(2,1)}, u32[]{:S(2)}, u32[]{:S(2)}) collective-permute-start(bf16[2,256,768]{2,1,0:T(8,128)(2,1)S(1)} %collective-permute-done), channel_id=1, source_target_pairs={{0,64},{64,128},{128,192},{192,256},{256,320},{320,384},{384,448},... | collective-permute-start | bytes 2359304 | tf_op jit(solution)/shard_map/ppermute | solution.py:25
  87.7 16.7 %collective-permute-start.3 = (bf16[2,256,768]{2,1,0:T(8,128)(2,1)S(1)}, bf16[2,256,768]{2,1,0:T(8,128)(2,1)}, u32[]{:S(2)}, u32[]{:S(2)}) collective-permute-start(bf16[2,256,768]{2,1,0:T(8,128)(2,1)S(1)} %collective-permute-done.1), channel_id=1, source_target_pairs={{0,448},{64,0},{128,64},{192,128},{256,192},{320,256},{384,320},{4... | collective-permute-start | bytes 2359304 | tf_op jit(solution)/shard_map/ppermute | solution.py:30
  100.4 12.9 %collective-permute-start.4 = (bf16[2,256,768]{2,1,0:T(8,128)(2,1)}, bf16[2,256,768]{2,1,0:T(8,128)(2,1)}, u32[]{:S(2)}, u32[]{:S(2)}) collective-permute-start(bf16[2,256,768]{2,1,0:T(8,128)(2,1)} %collective-permute-done.2), channel_id=1, source_target_pairs={{0,64},{64,128},{128,192},{192,256},{256,320},{320,384},{384,448},... | collective-permute-start | bytes 2359304 | tf_op jit(solution)/shard_map/ppermute | solution.py:25
  104.4 17.0 %collective-permute-start.5 = (bf16[2,256,768]{2,1,0:T(8,128)(2,1)}, bf16[2,256,768]{2,1,0:T(8,128)(2,1)S(1)}, u32[]{:S(2)}, u32[]{:S(2)}) collective-permute-start(bf16[2,256,768]{2,1,0:T(8,128)(2,1)} %collective-permute-done.3), channel_id=1, source_target_pairs={{0,448},{64,0},{128,64},{192,128},{256,192},{320,256},{384,320},{4... | collective-permute-start | bytes 2359304 | tf_op jit(solution)/shard_map/ppermute | solution.py:30
  113.3 12.8 %collective-permute-start.6 = (bf16[2,256,768]{2,1,0:T(8,128)(2,1)}, bf16[2,256,768]{2,1,0:T(8,128)(2,1)S(1)}, u32[]{:S(2)}, u32[]{:S(2)}) collective-permute-start(bf16[2,256,768]{2,1,0:T(8,128)(2,1)} %collective-permute-done.4), channel_id=1, source_target_pairs={{0,64},{64,128},{128,192},{192,256},{256,320},{320,384},{384,448},... | collective-permute-start | bytes 2359304 | tf_op jit(solution)/shard_map/ppermute | solution.py:25
Sparse Core Ops, SparseCore 0:
  458.8 31.8 reduce-scatter.1
